TPU v7x, 32 devices: a whole 2x2x4 slice. The times are simulated.
32 devices in a mesh: expert: 16 (over z, y, x), tok: 2 (over core).
Axes of the slice: x: 2, y: 2, z: 4, core: 2. Of those that a mesh axis runs over, the one named last changes fastest.
Arguments:
- tokens: bfloat16 [2048, 3584], P(('expert', 'tok')), may hold values from -6 to 6
- routes: int32 [2048, 8], P(('expert', 'tok')), may hold values from 0 to 15, all different within a row; in each aligned block of 64 rows (0 to 63, 64 to 127, ...) at most 36 rows name the same one
- gates: float32 [2048, 8], P(('expert', 'tok')), may hold values from 0.05 to 1
- upstream: bfloat16 [2048, 3584], P(('expert', 'tok')), may hold values from -6 to 6
- w_up: bfloat16 [16, 3584, 1024], P('expert', None, 'tok'), may hold values from -0.09375 to 0.09375
- w_down: bfloat16 [16, 1024, 3584], P('expert', 'tok'), may hold values from -0.1875 to 0.1875
Outputs:
- mixed: bfloat16 [2048, 3584], P(('expert', 'tok'))
- d_tokens: bfloat16 [2048, 3584], P(('expert', 'tok'))
- d_gates: float32 [2048, 8], P(('expert', 'tok'))
- grad_up: bfloat16 [16, 3584, 1024], P('expert', None, 'tok')
- grad_down: bfloat16 [16, 1024, 3584], P('expert', 'tok')
Inputs may be any that keep to these rules, and one draw needn't show every extreme that they name: `routes`: each token names 8 different experts. At most 36 of the 64 tokens of one device name the same expert, and in every draw the tokens of some device name some expert exactly 36 times.
All inputs are finite; a program needn't handle non-finite values.
Results may differ from a plain program's by a relative error of at most 0.0065.
Values may be sent and summed in bfloat16 or wider, within the bound.
A program may use at most 192 MiB of HBM per device.

v0:
```python
import jax
import jax.numpy as jnp
from jax import lax
from jax.sharding import PartitionSpec as P

GELU_C = 0.7978845608028654
GELU_A = 0.044715


def gelu_value(hidden):
    inner_arg = GELU_C * (hidden + GELU_A * hidden * hidden * hidden)
    return 0.5 * hidden * (1.0 + jnp.tanh(inner_arg))


def gelu_slope(hidden):
    tangent = jnp.tanh(GELU_C * (hidden + GELU_A * hidden * hidden * hidden))
    return 0.5 * (1.0 + tangent) + 0.5 * hidden * (1.0 - tangent * tangent) * GELU_C * (
        1.0 + 3.0 * GELU_A * hidden * hidden
    )


def expert_rows(rows_x, rows_grad, up_local, down_local):
    hidden = jnp.dot(rows_x, up_local, preferred_element_type=jnp.float32)
    active = gelu_value(hidden).astype(jnp.bfloat16)
    out_part = jnp.dot(active, down_local, preferred_element_type=jnp.float32)
    d_active = lax.dot_general(
        rows_grad, down_local, (((1,), (1,)), ((), ())), preferred_element_type=jnp.float32
    )
    d_hidden = (d_active * gelu_slope(hidden)).astype(jnp.bfloat16)
    dx_part = lax.dot_general(
        d_hidden, up_local, (((1,), (1,)), ((), ())), preferred_element_type=jnp.float32
    )
    grad_down = lax.dot_general(
        active, rows_grad, (((0,), (0,)), ((), ())), preferred_element_type=jnp.float32
    )
    grad_up = lax.dot_general(
        rows_x, d_hidden, (((0,), (0,)), ((), ())), preferred_element_type=jnp.float32
    )
    return (out_part, dx_part, grad_up, grad_down)


def routed_shards(tokens, routes, gates, upstream, w_up, w_down):
    tok_rows, feature_width = tokens.shape
    top_count = routes.shape[1]
    owners = lax.axis_size("expert")
    pair_count = lax.axis_size("tok")
    capacity = tok_rows * top_count // owners + max(1, tok_rows * top_count // (8 * owners))
    assigned = routes.reshape(-1)
    labels = jnp.arange(owners, dtype=jnp.int32)
    onehot = (assigned[:, None] == labels[None, :]).astype(jnp.int32)
    earlier = jnp.cumsum(onehot, axis=0) - onehot
    slot_rank = jnp.sum(earlier * onehot, axis=1)
    slot_of = assigned * capacity + slot_rank
    slot_ids = jnp.arange(owners * capacity, dtype=jnp.int32)
    matches = (slot_of[None, :] == slot_ids[:, None]).astype(jnp.int32)
    filled = jnp.sum(matches, axis=1) > 0
    source = jnp.sum(matches * jnp.arange(assigned.shape[0], dtype=jnp.int32)[None, :], axis=1)
    token_ids = source // top_count
    send_x = jnp.where(filled[:, None], tokens[token_ids], jnp.zeros((), jnp.bfloat16))
    gate_rows = jnp.where(filled, gates.reshape(-1)[source], jnp.zeros((), jnp.float32))
    send_grad = (gate_rows[:, None] * upstream[token_ids].astype(jnp.float32)).astype(jnp.bfloat16)
    send_x = send_x.reshape(owners, capacity, feature_width)
    send_grad = send_grad.reshape(owners, capacity, feature_width)
    recv_x, recv_grad = (
        lax.all_to_all(send_x, "expert", split_axis=0, concat_axis=0, tiled=True),
        lax.all_to_all(send_grad, "expert", split_axis=0, concat_axis=0, tiled=True),
    )
    both_x, both_grad = (
        lax.all_gather(recv_x[None], "tok", axis=0, tiled=True),
        lax.all_gather(recv_grad[None], "tok", axis=0, tiled=True),
    )
    rows_x = both_x.reshape(-1, feature_width)
    rows_grad = both_grad.reshape(-1, feature_width)
    out_part, dx_part, grad_up, grad_down = expert_rows(rows_x, rows_grad, w_up[0], w_down[0])
    shaped_out = out_part.reshape(pair_count, owners, capacity, feature_width)
    shaped_dx = dx_part.reshape(pair_count, owners, capacity, feature_width)
    summed_out, summed_dx = (
        lax.psum_scatter(shaped_out, "tok", scatter_dimension=0, tiled=True),
        lax.psum_scatter(shaped_dx, "tok", scatter_dimension=0, tiled=True),
    )
    home_out, home_dx = (
        lax.all_to_all(
            summed_out[0].astype(jnp.bfloat16), "expert", split_axis=0, concat_axis=0, tiled=True
        ),
        lax.all_to_all(
            summed_dx[0].astype(jnp.bfloat16), "expert", split_axis=0, concat_axis=0, tiled=True
        ),
    )
    out_pairs = (
        home_out.reshape(owners * capacity, feature_width)[slot_of]
        .reshape(tok_rows, top_count, feature_width)
        .astype(jnp.float32)
    )
    dx_pairs = (
        home_dx.reshape(owners * capacity, feature_width)[slot_of]
        .reshape(tok_rows, top_count, feature_width)
        .astype(jnp.float32)
    )
    mixed_out = jnp.sum(gates[:, :, None] * out_pairs, axis=1).astype(jnp.bfloat16)
    d_gates = jnp.sum(upstream.astype(jnp.float32)[:, None, :] * out_pairs, axis=2)
    d_tokens = jnp.sum(dx_pairs, axis=1).astype(jnp.bfloat16)
    return (
        mixed_out,
        d_tokens,
        d_gates,
        grad_up.astype(jnp.bfloat16)[None],
        grad_down.astype(jnp.bfloat16)[None],
    )


def dense_shards(tokens, routes, gates, upstream, w_up, w_down):
    tok_rows, width = tokens.shape
    owners = lax.axis_size("expert")
    half = w_up.shape[2]
    swap = ((0, 1), (1, 0))
    up_local, down_local = (w_up[0], w_down[0])
    up_full = jnp.concatenate([up_local, lax.ppermute(up_local, "tok", swap)], axis=1)
    down_full = jnp.concatenate([down_local, lax.ppermute(down_local, "tok", swap)], axis=0)
    named = routes[:, :, None] == jnp.arange(owners, dtype=jnp.int32)
    gate_of = jnp.sum(jnp.where(named, gates[:, :, None], 0.0), axis=1)
    gate = lax.all_to_all(gate_of.T, "expert", split_axis=0, concat_axis=0, tiled=True)
    gate = gate.reshape(-1)[:, None]
    all_x = lax.all_gather(tokens, "expert", axis=0, tiled=True)
    all_u = lax.all_gather(upstream, "expert", axis=0, tiled=True)
    hidden = jnp.dot(all_x, up_full, preferred_element_type=jnp.float32)
    gated = (gate * gelu_value(hidden)).astype(jnp.bfloat16)
    mixed_part = jnp.dot(gated, down_full, preferred_element_type=jnp.float32)
    mixed = lax.psum_scatter(
        mixed_part.astype(jnp.bfloat16), "expert", scatter_dimension=0, tiled=True
    )
    back = lax.dot_general(
        all_u, down_full, (((1,), (1,)), ((), ())), preferred_element_type=jnp.float32
    )
    inner = jnp.sum(gelu_value(hidden) * back, axis=1)
    d_hidden = (gate * back * gelu_slope(hidden)).astype(jnp.bfloat16)
    dx_part = lax.dot_general(
        d_hidden, up_full, (((1,), (1,)), ((), ())), preferred_element_type=jnp.float32
    )
    d_tokens = lax.psum_scatter(
        dx_part.astype(jnp.bfloat16), "expert", scatter_dimension=0, tiled=True
    )
    home = lax.all_to_all(
        inner.reshape(owners, tok_rows), "expert", split_axis=0, concat_axis=0, tiled=True
    )
    d_gates = jnp.sum(jnp.where(named, home.T[:, None, :], 0.0), axis=2)

    def outer(rows, columns):
        return lax.dot_general(
            rows, columns, (((0,), (0,)), ((), ())), preferred_element_type=jnp.float32
        )

    down_far = outer(gated[:, half:], all_u).astype(jnp.bfloat16)
    up_far = outer(all_x, d_hidden[:, half:]).astype(jnp.bfloat16)
    down_near = outer(gated[:, :half], all_u)
    up_near = outer(all_x, d_hidden[:, :half])
    grad_down = down_near + lax.ppermute(down_far, "tok", swap).astype(jnp.float32)
    grad_up = up_near + lax.ppermute(up_far, "tok", swap).astype(jnp.float32)
    return (
        mixed,
        d_tokens,
        d_gates,
        grad_up.astype(jnp.bfloat16)[None],
        grad_down.astype(jnp.bfloat16)[None],
    )


def shards(tokens, routes, gates, upstream, w_up, w_down):
    dense = 2 * routes.shape[1] >= lax.axis_size("expert") and lax.axis_size("tok") == 2
    body = dense_shards if dense else routed_shards
    return body(tokens, routes, gates, upstream, w_up, w_down)


def solution(mesh):
    return jax.shard_map(
        shards,
        mesh=mesh,
        in_specs=(
            P(("expert", "tok"), None),
            P(("expert", "tok"), None),
            P(("expert", "tok"), None),
            P(("expert", "tok"), None),
            P("expert", None, "tok"),
            P("expert", "tok", None),
        ),
        out_specs=(
            P(("expert", "tok"), None),
            P(("expert", "tok"), None),
            P(("expert", "tok"), None),
            P("expert", None, "tok"),
            P("expert", "tok", None),
        ),
        check_vma=False,
    )
```

profile of v0, /device:TPU:10, one launch (start us, length us, event | category | flops | bytes accessed | tf_op | source)
XLA Modules:
  0.0 600.3 jit_solution(6524580034297987019)
XLA Ops:
  7.2 0.7 all-gather.3.cloned.1.call-update
  7.9 0.7 all-gather.5.cloned.1.call-update
  8.8 0.5 collective-permute-start.1
  9.3 6.2 %collective-permute-done = bf16[3584,512]{1,0:T(8,128)(2,1)} collective-permute-done((bf16[3584,512]{1,0:T(8,128)(2,1)}, bf16[3584,512]{1,0:T(8,128)(2,1)}, u32[]{:S(2)}, u32[]{:S(2)}) %collective-permute-start) | collective-permute-done | bytes 3670048 | tf_op jit(solution)/shard_map/ppermute | solution.py:117
  15.5 98.8 %all-gather.3.cloned.1.call-done = bf16[1024,3584]{1,0:T(8,128)(2,1)} async-done(((bf16[64,3584]{1,0:T(8,128)(2,1)}), bf16[1024,3584]{1,0:T(8,128)(2,1)}) %all-gather.3.cloned.1.call-update) | async-done | bytes 7340048 | tf_op jit(solution)/shard_map/all_gather | solution.py:123
  114.3 13.6 %fusion.4 = f32[1024,1024]{1,0:T(8,128)} fusion(bf16[1024,3584]{1,0:T(8,128)(2,1)} %all-gather.3.cloned.1.call-done, bf16[3584,512]{1,0:T(8,128)(2,1)} %collective-permute-done, bf16[3584,512]{1,0:T(8,128)(2,1)} %bitcast.60), kind=kOutput, calls=%fused_computation.14 | convolution fusion | flops 7530872832 | bytes 18874368 | tf_op jit(solution)/shard_map/dot_general | solution.py:125
  127.9 90.8 %all-gather.5.cloned.1.call-done = bf16[1024,3584]{1,0:T(8,128)(2,1)} async-done(((bf16[64,3584]{1,0:T(8,128)(2,1)}), bf16[1024,3584]{1,0:T(8,128)(2,1)}) %all-gather.5.cloned.1.call-update) | async-done | bytes 7340048 | tf_op jit(solution)/shard_map/all_gather | solution.py:124
  218.7 15.0 %fusion.12 = (f32[1024]{0:T(1024)S(1)}, f32[1024,1024]{1,0:T(8,128)}) fusion(f32[1024,1024]{1,0:T(8,128)} %fusion.4, bf16[1024,3584]{1,0:T(8,128)(2,1)} %all-gather.5.cloned.1.call-done, bf16[512,3584]{1,0:T(8,128)(2,1)} %collective-permute-done.1, bf16[512,3584]{1,0:T(8,128)(2,1)} %bitcast.63), kind=kOutput, calls=%fused_computation.24 | convolution fusion | flops 7541357568 | bytes 23072768 | tf_op jit(solution)/shard_map/dot_general | solution.py:131
  233.7 10.0 %all_to_all.21 = f32[16,1,64]{2,1,0:T(1,128)S(1)} all-to-all(f32[16,1,64]{2,1,0:T(1,128)S(1)} %bitcast.56), channel_id=1, replica_groups=mesh['expert'=16,'tok'=2] {'expert'}, dimensions={0} | all-to-all | bytes 8192 | tf_op jit(solution)/shard_map/all_to_all | solution.py:142
  243.8 0.6 select_reduce_fusion
  244.4 9.8 %all_to_all.22 = f32[16,1,64]{2,1,0:T(1,128)S(1)} all-to-all(f32[16,1,64]{2,1,0:T(1,128)S(1)} %bitcast.55), channel_id=1, replica_groups=mesh['expert'=16,'tok'=2] {'expert'}, dimensions={0} | all-to-all | bytes 8192 | tf_op jit(solution)/shard_map/all_to_all | solution.py:121
  254.2 0.5 broadcast.46
  254.7 0.7 reduce.3
  255.5 5.6 fusion.11
  261.1 1.3 copy-done
  262.4 12.0 %convolution_convert_fusion = bf16[1024,3584]{1,0:T(8,128)(2,1)} fusion(bf16[1024,1024]{0,1:T(8,128)(2,1)S(1)} %get-tuple-element.27, bf16[3584,512]{1,0:T(8,128)(2,1)} %collective-permute-done, bf16[3584,512]{1,0:T(8,128)(2,1)S(1)} %bitcast.61), kind=kOutput, calls=%fused_computation | convolution fusion | flops 7534542848 | bytes 16777216 | tf_op jit(solution)/shard_map/dot_general | solution.py:136
  274.6 13.0 %convolution_convert_fusion.1 = bf16[1024,3584]{1,0:T(8,128)(2,1)} fusion(bf16[1024,1024]{0,1:T(8,128)(2,1)S(1)} %get-tuple-element.28, bf16[512,3584]{1,0:T(8,128)(2,1)} %collective-permute-done.1, bf16[512,3584]{1,0:T(8,128)(2,1)} %bitcast.64), kind=kOutput, calls=%fused_computation.1 | convolution fusion | flops 7534542848 | bytes 16777216 | tf_op jit(solution)/shard_map/dot_general | solution.py:127
  287.7 7.5 %fusion.1 = bf16[3584,512]{0,1:T(8,128)(2,1)S(1)} fusion(bf16[1024,3584]{1,0:T(8,128)(2,1)} %all-gather.3.cloned.1.call-done, bf16[1024,1024]{0,1:T(8,128)(2,1)} %copy-done), kind=kOutput, calls=%fused_computation.11 | convolution fusion | flops 3759931392 | bytes 12058624 | tf_op jit(solution)/shard_map/dot_general | solution.py:148
  295.4 8.7 %convolution_convert_fusion.2 = bf16[512,3584]{1,0:T(8,128)(2,1)} fusion(bf16[1024,3584]{1,0:T(8,128)(2,1)} %all-gather.5.cloned.1.call-done, bf16[1024,1024]{0,1:T(8,128)(2,1)S(1)} %get-tuple-element.28), kind=kOutput, calls=%fused_computation.9 | convolution fusion | flops 3759931392 | bytes 12058624 | tf_op jit(solution)/shard_map/dot_general | solution.py:148
  304.4 5.4 fusion.2
  309.8 5.9 copy.25
  315.7 9.1 %fusion.14 = bf16[1,512,3584]{2,1,0:T(8,128)(2,1)} fusion(bf16[512,3584]{1,0:T(8,128)(2,1)} %collective-permute-done.3, bf16[1024,3584]{1,0:T(8,128)(2,1)} %all-gather.5.cloned.1.call-done, bf16[1024,1024]{0,1:T(8,128)(2,1)S(1)} %get-tuple-element.28), kind=kOutput, calls=%fused_computation.28 | convolution fusion | flops 3763601408 | bytes 15728640 | tf_op jit(solution)/shard_map/dot_general | solution.py:148
  324.8 107.0 %reduce-scatter.5.cloned.1.call-done = bf16[64,3584]{1,0:T(8,128)(2,1)} async-done(((bf16[1024,3584]{1,0:T(8,128)(2,1)}), bf16[64,3584]{1,0:T(8,128)(2,1)}) %reduce-scatter.5.cloned.1.call-update) | async-done | bytes 458768 | tf_op jit(solution)/shard_map/reduce_scatter | solution.py:139
  431.8 161.9 %reduce-scatter.3.cloned.1.call-done = bf16[64,3584]{1,0:T(8,128)(2,1)} async-done(((bf16[1024,3584]{1,0:T(8,128)(2,1)}), bf16[64,3584]{1,0:T(8,128)(2,1)}) %reduce-scatter.3.cloned.1.call-update) | async-done | bytes 458768 | tf_op jit(solution)/shard_map/reduce_scatter | solution.py:128
  (28 shorter events, 1.0 us)
Async XLA Ops:
  7.2 107.2 %all-gather.3.cloned.1.call-start = ((), (), s32[]{:S(2)}) async-start(), calls=%async_computation.4 | async-start | bytes 7798784 | tf_op jit(solution)/shard_map/all_gather | solution.py:123
  7.9 210.8 %all-gather.5.cloned.1.call-start = ((), (), s32[]{:S(2)}) async-start(), calls=%async_computation.6 | async-start | bytes 7798784 | tf_op jit(solution)/shard_map/all_gather | solution.py:124
  8.6 423.2 %reduce-scatter.5.cloned.1.call-start = ((), (), s32[]{:S(2)}) async-start(), calls=%async_computation.7 | async-start | bytes 7798784 | tf_op jit(solution)/shard_map/reduce_scatter | solution.py:139
  8.7 6.8 %collective-permute-start = (bf16[3584,512]{1,0:T(8,128)(2,1)}, bf16[3584,512]{1,0:T(8,128)(2,1)}, u32[]{:S(2)}, u32[]{:S(2)}) collective-permute-start(bf16[3584,512]{1,0:T(8,128)(2,1)} %bitcast.59), channel_id=1, source_target_pairs={{0,1},{1,0},{2,3},{3,2},{4,5},{5,4},{6,7},{7,6},{8,9},{9,8},{10,11... | collective-permute-start | bytes 11010056 | tf_op jit(solution)/shard_map/ppermute | solution.py:117
  8.8 119.1 %collective-permute-start.1 = (bf16[512,3584]{1,0:T(8,128)(2,1)}, bf16[512,3584]{1,0:T(8,128)(2,1)}, u32[]{:S(2)}, u32[]{:S(2)}) collective-permute-start(bf16[512,3584]{1,0:T(8,128)(2,1)} %bitcast.62), channel_id=1, source_target_pairs={{0,1},{1,0},{2,3},{3,2},{4,5},{5,4},{6,7},{7,6},{8,9},{9,8},{10,11... | collective-permute-start | bytes 11010056 | tf_op jit(solution)/shard_map/ppermute | solution.py:118
  127.9 115.9 %copy-start.2 = (s32[64,8]{0,1:T(8,128)S(1)}, s32[64,8]{0,1:T(8,128)}, u32[]{:S(2)}) copy-start(s32[64,8]{0,1:T(8,128)} %param.7) | copy-start | bytes 6148
  127.9 115.9 %copy-start.3 = (f32[64,8]{0,1:T(8,128)S(1)}, f32[64,8]{0,1:T(8,128)}, u32[]{:S(2)}) copy-start(f32[64,8]{0,1:T(8,128)} %param.8) | copy-start | bytes 6148
  255.5 6.9 %copy-start.4 = (bf16[1,3584,512]{2,1,0:T(8,128)(2,1)S(1)}, bf16[1,3584,512]{2,1,0:T(8,128)(2,1)}, u32[]{:S(2)}) copy-start(bf16[1,3584,512]{2,1,0:T(8,128)(2,1)} %param.10) | copy-start | bytes 11010052
  261.1 1.3 copy-start
  274.4 319.4 %reduce-scatter.3.cloned.1.call-start = ((), (), s32[]{:S(2)}) async-start(), calls=%async_computation.5 | async-start | bytes 7798784 | tf_op jit(solution)/shard_map/reduce_scatter | solution.py:128
  287.7 16.6 %slice-start = ((s8[7340032]{0:T(1024)(128)(4,1)}), s8[4194304]{0:T(1024)(128)(4,1)S(1)}, s32[]{:S(2)}) async-start(s8[7340032]{0:T(1024)(128)(4,1)} %bitcast.57), calls=%async_computation.8 | async-start | bytes 8388608
  295.3 9.1 %copy-start.1 = (bf16[1024,1024]{0,1:T(8,128)(2,1)S(1)}, bf16[1024,1024]{0,1:T(8,128)(2,1)}, u32[]{:S(2)}) copy-start(bf16[1024,1024]{0,1:T(8,128)(2,1)} %copy-done) | copy-start | bytes 6291460
  295.3 9.1 %slice-start.1 = ((s8[7340032]{0:T(1024)(128)(4,1)}), s8[3145728]{0:T(1024)(128)(4,1)S(1)}, s32[]{:S(2)}) async-start(s8[7340032]{0:T(1024)(128)(4,1)} %bitcast.57), calls=%async_computation.9 | async-start | bytes 6291456
  295.3 9.1 %collective-permute-start.2 = (bf16[3584,512]{0,1:T(8,128)(2,1)S(1)}, bf16[3584,512]{0,1:T(8,128)(2,1)S(1)}, u32[]{:S(2)}, u32[]{:S(2)}) collective-permute-start(bf16[3584,512]{0,1:T(8,128)(2,1)S(1)} %fusion.1), channel_id=1, source_target_pairs={{0,1},{1,0},{2,3},{3,2},{4,5},{5,4},{6,7},{7,6},{8,9},{9,8},{10,11... | collective-permute-start | bytes 11010056 | tf_op jit(solution)/shard_map/ppermute | solution.py:157
  304.0 11.7 %collective-permute-start.3 = (bf16[512,3584]{1,0:T(8,128)(2,1)}, bf16[512,3584]{1,0:T(8,128)(2,1)}, u32[]{:S(2)}, u32[]{:S(2)}) collective-permute-start(bf16[512,3584]{1,0:T(8,128)(2,1)} %convolution_convert_fusion.2), channel_id=1, source_target_pairs={{0,1},{1,0},{2,3},{3,2},{4,5},{5,4},{6,7},{7,6},{8,9},{9,8},{10,11... | collective-permute-start | bytes 11010056 | tf_op jit(solution)/shard_map/ppermute | solution.py:156
Sparse Core Ops, SparseCore 0:
  10.7 103.6 all-gather.2
  117.0 101.6 all-gather.4
  274.5 157.2 reduce-scatter.4
  434.6 159.1 reduce-scatter.2
where the time goes:
time: 601 us; the launch traced here: 600 us
  waiting for transfers between devices  466 us (78%)
  matrix products  84.3 us (14%)
  blocking collectives  19.9 us (3%)
  between operations  13.9 us (2%)
  local copies, waits for them, and re-layouts  7.92 us (1%)
  other arithmetic  6.87 us (1%)
    reduce_scatter x1, waiting for transfers between devices, dense_shards(): lax.psum_scatter(mixed_part.astype(jnp.bfloat16), 'expert', scatter_dimen...  162 us
    reduce_scatter x1, waiting for transfers between devices, dense_shards(): lax.psum_scatter(dx_part.astype(jnp.bfloat16), 'expert', scatter_dimensio...  107 us
    all_gather x1, waiting for transfers between devices, dense_shards(): all_x = lax.all_gather(tokens, 'expert', axis=0, tiled=True)  98.8 us
    all_gather x1, waiting for transfers between devices, dense_shards(): all_u = lax.all_gather(upstream, 'expert', axis=0, tiled=True)  90.8 us
    dot_general x4, matrix products, outer(): lax.dot_general(rows, columns, (((0,), (0,)), ((), ())), preferred_elemen...  30.7 us
    dot_general x1, matrix products, dense_shards(): lax.dot_general(all_u, down_full, (((1,), (1,)), ((), ())), preferred_ele...  15 us
    dot_general x1, matrix products, dense_shards(): hidden = jnp.dot(all_x, up_full, preferred_element_type=jnp.float32)  13.6 us
    dot_general x1, matrix products, dense_shards(): mixed_part = jnp.dot(gated, down_full, preferred_element_type=jnp.float32)  13 us
  transfers between devices with their start and end apart: 8, of which 5 were waited for; matrix products, arithmetic and copies ran while one was open for 11% of the time, Pallas kernels for 0%

commit v1 on v0

--- a/solution.py
+++ b/solution.py
@@ -5,6 +5,18 @@
 
 GELU_C = 0.7978845608028654
 GELU_A = 0.044715
+
+
+def doubled_up(shard, axis, dim):
+    ways, here = (lax.axis_size(axis), lax.axis_index(axis))
+    grown, reach = (shard, 1)
+    while reach < ways:
+        theirs = lax.ppermute(grown, axis, [(d, d ^ reach) for d in range(ways)])
+        mine_first = jnp.concatenate([grown, theirs], axis=dim)
+        theirs_first = jnp.concatenate([theirs, grown], axis=dim)
+        grown = jnp.where(here & reach == 0, mine_first, theirs_first)
+        reach = 2 * reach
+    return grown
 
 
 def gelu_value(hidden):
@@ -120,7 +132,7 @@
     gate_of = jnp.sum(jnp.where(named, gates[:, :, None], 0.0), axis=1)
     gate = lax.all_to_all(gate_of.T, "expert", split_axis=0, concat_axis=0, tiled=True)
     gate = gate.reshape(-1)[:, None]
-    all_x = lax.all_gather(tokens, "expert", axis=0, tiled=True)
+    all_x = doubled_up(tokens, "expert", 0)
     all_u = lax.all_gather(upstream, "expert", axis=0, tiled=True)
     hidden = jnp.dot(all_x, up_full, preferred_element_type=jnp.float32)
     gated = (gate * gelu_value(hidden)).astype(jnp.bfloat16)

time: 601 us -> 702 us (1.17)
  waiting for transfers between devices: 466 us -> 555 us
  other arithmetic: 6.87 us -> 15.1 us
  local copies, waits for them, and re-layouts: 7.92 us -> 0.67 us
    ppermute x0 -> x4, waiting for transfers between devices: none -> 282 us  [doubled_up(): theirs = lax.ppermute(grown, axis, [(d, d ^ reach) for d in range(ways)])]
    all_gather x1 -> x0, waiting for transfers between devices: 98.8 us -> none  [dense_shards(): all_x = lax.all_gather(tokens, 'expert', axis=0, tiled=True)]
    all_gather x1, waiting for transfers between devices: 90.8 us -> 0.02 us  [dense_shards(): all_u = lax.all_gather(upstream, 'expert', axis=0, tiled=True)]
    unnamed x15 -> x12, local copies, waits for them, and re-layouts: 7.26 us -> 0.02 us
    select_n x0 -> x3, other arithmetic: none -> 7.19 us  [doubled_up(): grown = jnp.where(here & reach == 0, mine_first, theirs_first)]
  transfers between devices with their start and end apart: 8 -> 11, of which waited for: 5 -> 7; matrix products, arithmetic and copies ran while one was open for 11% -> 10% of each run, Pallas kernels for 0% -> 0%
where the time goes in v1:
time: 702 us
  waiting for transfers between devices  555 us (79%)
  matrix products  87.4 us (12%)
  blocking collectives  22.6 us (3%)
  other arithmetic  15.1 us (2%)
  between operations  13.8 us (2%)
    ppermute x4, waiting for transfers between devices, doubled_up(): theirs = lax.ppermute(grown, axis, [(d, d ^ reach) for d in range(ways)])  282 us
    reduce_scatter x1, waiting for transfers between devices, dense_shards(): lax.psum_scatter(mixed_part.astype(jnp.bfloat16), 'expert', scatter_dimen...  162 us
    reduce_scatter x1, waiting for transfers between devices, dense_shards(): lax.psum_scatter(dx_part.astype(jnp.bfloat16), 'expert', scatter_dimensio...  110 us
    dot_general x4, matrix products, outer(): lax.dot_general(rows, columns, (((0,), (0,)), ((), ())), preferred_elemen...  33.3 us
    dot_general x1, matrix products, dense_shards(): lax.dot_general(all_u, down_full, (((1,), (1,)), ((), ())), preferred_ele...  14.8 us
    dot_general x1, matrix products, dense_shards(): hidden = jnp.dot(all_x, up_full, preferred_element_type=jnp.float32)  14.6 us
  transfers between devices with their start and end apart: 11, of which 7 were waited for; matrix products, arithmetic and copies ran while one was open for 10% of the time, Pallas kernels for 0%

profile of v1, /device:TPU:10, one launch (start us, length us, event | category | flops | bytes accessed | tf_op | source)
XLA Modules:
  0.0 701.7 jit_solution(11287858426783208429)
XLA Ops:
  7.2 0.7 all-gather.2.cloned.1.call-update
  8.5 11.9 %collective-permute-done = bf16[64,3584]{1,0:T(8,128)(2,1)S(1)} collective-permute-done((bf16[64,3584]{1,0:T(8,128)(2,1)}, bf16[64,3584]{1,0:T(8,128)(2,1)S(1)}, u32[]{:S(2)}, u32[]{:S(2)}) %collective-permute-start) | collective-permute-done | bytes 458784 | tf_op jit(solution)/shard_map/ppermute | solution.py:14
  20.5 1.4 maximum_select_fusion.3
  21.9 1.6 collective-permute-start.1
  23.4 25.4 %collective-permute-done.1 = bf16[128,3584]{1,0:T(8,128)(2,1)} collective-permute-done((bf16[128,3584]{1,0:T(8,128)(2,1)S(1)}, bf16[128,3584]{1,0:T(8,128)(2,1)}, u32[]{:S(2)}, u32[]{:S(2)}) %collective-permute-start.1) | collective-permute-done | bytes 917536 | tf_op jit(solution)/shard_map/ppermute | solution.py:14
  48.8 1.9 maximum_select_fusion.2
  51.3 88.8 %collective-permute-done.2 = bf16[256,3584]{1,0:T(8,128)(2,1)} collective-permute-done((bf16[256,3584]{1,0:T(8,128)(2,1)S(1)}, bf16[256,3584]{1,0:T(8,128)(2,1)}, u32[]{:S(2)}, u32[]{:S(2)}) %collective-permute-start.2) | collective-permute-done | bytes 1835040 | tf_op jit(solution)/shard_map/ppermute | solution.py:14
  140.1 3.9 maximum_select_fusion.1
  144.0 3.3 collective-permute-start.3
  147.4 155.6 %collective-permute-done.3 = bf16[512,3584]{1,0:T(8,128)(2,1)} collective-permute-done((bf16[512,3584]{1,0:T(8,128)(2,1)}, bf16[512,3584]{1,0:T(8,128)(2,1)}, u32[]{:S(2)}, u32[]{:S(2)}) %collective-permute-start.3) | collective-permute-done | bytes 3670048 | tf_op jit(solution)/shard_map/ppermute | solution.py:14
  302.9 14.6 %fusion.2 = f32[1024,1024]{0,1:T(8,128)} fusion(bf16[3584,512]{1,0:T(8,128)(2,1)} %collective-permute-done.4, bf16[3584,512]{1,0:T(8,128)(2,1)} %bitcast.33, bf16[512,3584]{1,0:T(8,128)(2,1)} %collective-permute-done.3, bf16[512,3584]{1,0:T(8,128)(2,1)} %maximum_select_fusion.1, pred[]{:T(512)S(6)} %eq.28), kind=kOutput, calls=%fused_computation.13 | convolution fusion | flops 7563902976 | bytes 18874368 | tf_op jit(solution)/shard_map/dot_general | solution.py:137
  317.6 14.8 %fusion.10 = (f32[1024]{0:T(1024)S(1)}, f32[1024,1024]{1,0:T(8,128)}) fusion(f32[1024,1024]{0,1:T(8,128)} %fusion.2, bf16[1024,3584]{1,0:T(8,128)(2,1)} %all-gather.2.cloned.1.call-done, bf16[512,3584]{1,0:T(8,128)(2,1)} %collective-permute-done.5, bf16[512,3584]{1,0:T(8,128)(2,1)} %bitcast.4), kind=kOutput, calls=%fused_computation.23 | convolution fusion | flops 7541357568 | bytes 23072768 | tf_op jit(solution)/shard_map/dot_general | solution.py:143
  332.5 12.8 %all_to_all.21 = f32[16,1,64]{2,1,0:T(1,128)S(1)} all-to-all(f32[16,1,64]{2,1,0:T(1,128)S(1)} %bitcast.29), channel_id=1, replica_groups=mesh['expert'=16,'tok'=2] {'expert'}, dimensions={0} | all-to-all | bytes 8192 | tf_op jit(solution)/shard_map/all_to_all | solution.py:154
  345.9 9.8 %all_to_all.22 = f32[16,1,64]{2,1,0:T(1,128)S(1)} all-to-all(f32[16,1,64]{2,1,0:T(1,128)S(1)} %bitcast.28), channel_id=1, replica_groups=mesh['expert'=16,'tok'=2] {'expert'}, dimensions={0} | all-to-all | bytes 8192 | tf_op jit(solution)/shard_map/all_to_all | solution.py:133
  357.0 6.6 fusion.9
  363.6 12.0 %convolution_convert_fusion = bf16[1024,3584]{1,0:T(8,128)(2,1)} fusion(bf16[1024,1024]{0,1:T(8,128)(2,1)S(1)} %get-tuple-element.7, bf16[3584,512]{1,0:T(8,128)(2,1)} %collective-permute-done.4, bf16[3584,512]{1,0:T(8,128)(2,1)S(1)} %bitcast.34), kind=kOutput, calls=%fused_computation | convolution fusion | flops 7534542848 | bytes 16777216 | tf_op jit(solution)/shard_map/dot_general | solution.py:148
  375.9 12.7 %convolution_convert_fusion.1 = bf16[1024,3584]{1,0:T(8,128)(2,1)} fusion(bf16[1024,1024]{0,1:T(8,128)(2,1)} %get-tuple-element.8, bf16[512,3584]{1,0:T(8,128)(2,1)} %collective-permute-done.5, bf16[512,3584]{1,0:T(8,128)(2,1)} %bitcast.4), kind=kOutput, calls=%fused_computation.1 | convolution fusion | flops 7534542848 | bytes 16777216 | tf_op jit(solution)/shard_map/dot_general | solution.py:139
  388.7 9.4 %convolution_convert_fusion.2 = bf16[512,3584]{1,0:T(8,128)(2,1)} fusion(bf16[1024,3584]{1,0:T(8,128)(2,1)} %all-gather.2.cloned.1.call-done, bf16[1024,1024]{0,1:T(8,128)(2,1)} %get-tuple-element.8), kind=kOutput, calls=%fused_computation.9 | convolution fusion | flops 3759931392 | bytes 12058624 | tf_op jit(solution)/shard_map/dot_general | solution.py:160
  398.1 9.1 %convolution_convert_fusion.3 = bf16[3584,512]{1,0:T(8,128)(2,1)} fusion(bf16[1024,1024]{0,1:T(8,128)(2,1)S(1)} %get-tuple-element.7, bf16[512,3584]{1,0:T(8,128)(2,1)} %collective-permute-done.3, bf16[512,3584]{1,0:T(8,128)(2,1)} %maximum_select_fusion.1, pred[]{:T(512)S(6)} %eq.28), kind=kOutput, calls=%fused_computation.10 | convolution fusion | flops 3792961536 | bytes 12058625 | tf_op jit(solution)/shard_map/dot_general | solution.py:160
  407.7 5.4 fusion.11
  413.1 0.8 collective-permute-done.6
  413.9 9.3 %fusion = bf16[1,3584,512]{2,1,0:T(8,128)(2,1)} fusion(bf16[3584,512]{1,0:T(8,128)(2,1)S(1)} %collective-permute-done.6, bf16[1024,1024]{0,1:T(8,128)(2,1)S(1)} %get-tuple-element.7, bf16[512,3584]{1,0:T(8,128)(2,1)} %collective-permute-done.3, bf16[512,3584]{1,0:T(8,128)(2,1)} %maximum_select_fusion.1, pred[]{:T(512)S(6)} %eq.28), kind=kOutput, calls=%fused_computation.11 | convolution fusion | flops 3796631552 | bytes 15728641 | tf_op jit(solution)/shard_map/dot_general | solution.py:160
  423.3 109.9 %reduce-scatter.5.cloned.1.call-done = bf16[64,3584]{1,0:T(8,128)(2,1)} async-done(((bf16[1024,3584]{1,0:T(8,128)(2,1)}), bf16[64,3584]{1,0:T(8,128)(2,1)}) %reduce-scatter.5.cloned.1.call-update) | async-done | bytes 458768 | tf_op jit(solution)/shard_map/reduce_scatter | solution.py:151
  533.1 162.1 %reduce-scatter.3.cloned.1.call-done = bf16[64,3584]{1,0:T(8,128)(2,1)} async-done(((bf16[1024,3584]{1,0:T(8,128)(2,1)}), bf16[64,3584]{1,0:T(8,128)(2,1)}) %reduce-scatter.3.cloned.1.call-update) | async-done | bytes 458768 | tf_op jit(solution)/shard_map/reduce_scatter | solution.py:140
  (33 shorter events, 4.0 us)
Async XLA Ops:
  7.2 310.4 %all-gather.2.cloned.1.call-start = ((), (), s32[]{:S(2)}) async-start(), calls=%async_computation.5 | async-start | bytes 7798784 | tf_op jit(solution)/shard_map/all_gather | solution.py:136
  7.9 525.2 %reduce-scatter.5.cloned.1.call-start = ((), (), s32[]{:S(2)}) async-start(), calls=%async_computation.6 | async-start | bytes 7798784 | tf_op jit(solution)/shard_map/reduce_scatter | solution.py:151
  7.9 12.5 %collective-permute-start = (bf16[64,3584]{1,0:T(8,128)(2,1)}, bf16[64,3584]{1,0:T(8,128)(2,1)S(1)}, u32[]{:S(2)}, u32[]{:S(2)}) collective-permute-start(bf16[64,3584]{1,0:T(8,128)(2,1)} %param.6), channel_id=1, source_target_pairs={{0,2},{2,0},{4,6},{6,4},{8,10},{10,8},{12,14},{14,12},{16,18},{18,... | collective-permute-start | bytes 1376264 | tf_op jit(solution)/shard_map/ppermute | solution.py:14
  21.9 27.0 %collective-permute-start.1 = (bf16[128,3584]{1,0:T(8,128)(2,1)S(1)}, bf16[128,3584]{1,0:T(8,128)(2,1)}, u32[]{:S(2)}, u32[]{:S(2)}) collective-permute-start(bf16[128,3584]{1,0:T(8,128)(2,1)S(1)} %maximum_select_fusion.3), channel_id=1, source_target_pairs={{0,4},{2,6},{4,0},{6,2},{8,12},{10,14},{12,8},{14,10},{16,20},{18,... | collective-permute-start | bytes 2752520 | tf_op jit(solution)/shard_map/ppermute | solution.py:14
  50.8 89.3 %collective-permute-start.2 = (bf16[256,3584]{1,0:T(8,128)(2,1)S(1)}, bf16[256,3584]{1,0:T(8,128)(2,1)}, u32[]{:S(2)}, u32[]{:S(2)}) collective-permute-start(bf16[256,3584]{1,0:T(8,128)(2,1)S(1)} %maximum_select_fusion.2), channel_id=1, source_target_pairs={{0,8},{2,10},{4,12},{6,14},{8,0},{10,2},{12,4},{14,6},{16,24},{18,... | collective-permute-start | bytes 5505032 | tf_op jit(solution)/shard_map/ppermute | solution.py:14
  51.3 96.0 %collective-permute-start.4 = (bf16[3584,512]{1,0:T(8,128)(2,1)}, bf16[3584,512]{1,0:T(8,128)(2,1)}, u32[]{:S(2)}, u32[]{:S(2)}) collective-permute-start(bf16[3584,512]{1,0:T(8,128)(2,1)} %bitcast.32), channel_id=1, source_target_pairs={{0,1},{1,0},{2,3},{3,2},{4,5},{5,4},{6,7},{7,6},{8,9},{9,8},{10,11... | collective-permute-start | bytes 11010056 | tf_op jit(solution)/shard_map/ppermute | solution.py:129
  144.0 158.9 %collective-permute-start.3 = (bf16[512,3584]{1,0:T(8,128)(2,1)}, bf16[512,3584]{1,0:T(8,128)(2,1)}, u32[]{:S(2)}, u32[]{:S(2)}) collective-permute-start(bf16[512,3584]{1,0:T(8,128)(2,1)} %maximum_select_fusion.1), channel_id=1, source_target_pairs={{0,16},{2,18},{4,20},{6,22},{8,24},{10,26},{12,28},{14,30},{16,0},... | collective-permute-start | bytes 11010056 | tf_op jit(solution)/shard_map/ppermute | solution.py:14
  147.3 170.2 %collective-permute-start.5 = (bf16[512,3584]{1,0:T(8,128)(2,1)}, bf16[512,3584]{1,0:T(8,128)(2,1)}, u32[]{:S(2)}, u32[]{:S(2)}) collective-permute-start(bf16[512,3584]{1,0:T(8,128)(2,1)} %bitcast.4), channel_id=1, source_target_pairs={{0,1},{1,0},{2,3},{3,2},{4,5},{5,4},{6,7},{7,6},{8,9},{9,8},{10,11... | collective-permute-start | bytes 11010056 | tf_op jit(solution)/shard_map/ppermute | solution.py:130
  317.5 27.8 %copy-start.1 = (s32[64,8]{0,1:T(8,128)S(1)}, s32[64,8]{0,1:T(8,128)}, u32[]{:S(2)}) copy-start(s32[64,8]{0,1:T(8,128)} %param.7) | copy-start | bytes 6148
  317.5 27.8 %copy-start.2 = (f32[64,8]{0,1:T(8,128)S(1)}, f32[64,8]{0,1:T(8,128)}, u32[]{:S(2)}) copy-start(f32[64,8]{0,1:T(8,128)} %param.8) | copy-start | bytes 6148
  357.0 6.6 copy-start.3
  375.7 319.5 %reduce-scatter.3.cloned.1.call-start = ((), (), s32[]{:S(2)}) async-start(), calls=%async_computation.4 | async-start | bytes 7798784 | tf_op jit(solution)/shard_map/reduce_scatter | solution.py:140
  388.6 19.1 %slice-start = ((s8[7340032]{0:T(1024)(128)(4,1)}), s8[4194304]{0:T(1024)(128)(4,1)S(1)}, s32[]{:S(2)}) async-start(s8[7340032]{0:T(1024)(128)(4,1)} %bitcast.30), calls=%async_computation.7 | async-start | bytes 8388608
  398.0 9.7 %copy-start = (bf16[1024,1024]{0,1:T(8,128)(2,1)S(1)}, bf16[1024,1024]{0,1:T(8,128)(2,1)}, u32[]{:S(2)}) copy-start(bf16[1024,1024]{0,1:T(8,128)(2,1)} %get-tuple-element.8) | copy-start | bytes 6291460
  398.0 9.7 %slice-start.1 = ((s8[7340032]{0:T(1024)(128)(4,1)}), s8[3145728]{0:T(1024)(128)(4,1)S(1)}, s32[]{:S(2)}) async-start(s8[7340032]{0:T(1024)(128)(4,1)} %bitcast.30), calls=%async_computation.8 | async-start | bytes 6291456
  398.0 9.6 %collective-permute-start.7 = (bf16[512,3584]{1,0:T(8,128)(2,1)}, bf16[512,3584]{1,0:T(8,128)(2,1)S(1)}, u32[]{:S(2)}, u32[]{:S(2)}) collective-permute-start(bf16[512,3584]{1,0:T(8,128)(2,1)} %convolution_convert_fusion.2), channel_id=1, source_target_pairs={{0,1},{1,0},{2,3},{3,2},{4,5},{5,4},{6,7},{7,6},{8,9},{9,8},{10,11... | collective-permute-start | bytes 11010056 | tf_op jit(solution)/shard_map/ppermute | solution.py:168
  407.2 6.7 collective-permute-start.6
Sparse Core Ops, SparseCore 0:
  10.7 132.1 all-gather.1
  375.8 157.2 reduce-scatter.4
  536.0 159.1 reduce-scatter.2
